TPU v7x, 256 devices: a whole 4x4x8 slice. The times are simulated.
256 devices in a mesh: cluster: 16 (over x, y), sub: 16 (over z, core).
Axes of the slice: x: 4, y: 4, z: 8, core: 2. Of those that a mesh axis runs over, the one named last changes fastest.
Arguments:
- dual_ops: float32 [16, 16, 1408, 1408], P('cluster', 'sub'), may hold values from -1 to 4.5, as said below
- contributions: float32 [16, 16, 1408, 64], P('cluster', 'sub'), may hold values from -6 to 6
- block_sizes: int32 [16, 16, 4], P('cluster', 'sub'), may hold values from 0 to 352, as said below
- mult_map: int32 [16, 16, 1408], P('cluster', 'sub'), may hold values from 0 to 1407, each once within a row
- coarse_basis: float32 [16, 16, 32, 704], P('cluster', 'sub'), may hold values from -0.21875 to 0.21875
- coarse_inverse: float32 [16, 512, 512], P('cluster'), may hold values from -0.1 to 0.5, as said below
Outputs:
- solution: float32 [16, 16, 1408, 64], P('cluster', 'sub')
- residual: float32 [16, 16, 1408, 64], P('cluster', 'sub')
Inputs may be any that keep to these rules, and one draw needn't show every extreme that they name: `dual_ops`: symmetric positive definite for each subdomain. block_sizes[c, s, k] equals the count on the facing side of the neighbour across side k; sides at the ends of an axis hold 0, all others 352 // 4 to 352; some side holds exactly 352. `mult_map`: for each subdomain a permutation of the 1408 slots. `coarse_inverse`: symmetric for each cluster.
All inputs are finite; a program needn't handle non-finite values.
Results may differ from a plain program's by a relative error of at most 0.0003.
Values sent between devices are 32-bit elements; how exact they have to be, the bound alone decides.
A program may use at most 64 MiB of HBM per device.

v0:
```python
import jax
import jax.numpy as jnp
from jax import lax
from jax.sharding import PartitionSpec as P

ITERS = 2
precise = lax.Precision.HIGHEST


def extended(value, sides, width):
    for axis, dim in sides:
        peers, length = (lax.axis_size(axis), value.shape[dim])
        up = [(i, (i + 1) % peers) for i in range(peers - 1)]
        down = [(j, i) for i, j in up]
        last = lax.slice_in_dim(value, length - width, length, axis=dim)
        leading = lax.slice_in_dim(value, 0, width, axis=dim)
        before = lax.ppermute(last, axis, up)
        after = lax.ppermute(leading, axis, down)
        value = jnp.concatenate([before, value, after], axis=dim)
    return value


def products(left, right):
    return lax.dot_general(
        left, right, (((0,), (0,)), ((), ())), precision=precise, preferred_element_type=jnp.float32
    )


def matmul(left, right):
    return jnp.dot(left, right, precision=precise, preferred_element_type=jnp.float32)


def chol_solve(factor, target):
    middle = lax.linalg.triangular_solve(factor, target, left_side=True, lower=True)
    return lax.linalg.triangular_solve(factor, middle, left_side=True, lower=True, transpose_a=True)


def join_pair(side_pair, padded):
    return jnp.stack([side_pair[0] + padded[0], side_pair[1] + padded[3]])


def shards(dual_ops, contributions, block_sizes, mult_map, coarse_basis, coarse_inverse):
    operator = dual_ops[0, 0]
    local_rhs = contributions[0, 0]
    side_sizes = block_sizes[0, 0]
    slot_map = mult_map[0, 0]
    basis_rows = coarse_basis[0, 0]
    coarse_matrix = coarse_inverse[0]
    orders = operator.shape[0]
    face_rows = orders // 4
    mode_count = basis_rows.shape[0]
    columns = local_rhs.shape[1]
    row_index = jnp.arange(orders, dtype=jnp.int32)
    row_side = row_index // face_rows
    row_place = row_index % face_rows
    side_match = row_side[:, None] == jnp.arange(4, dtype=jnp.int32)[None, :]
    row_limit = jnp.sum(jnp.where(side_match, side_sizes[None, :], 0), axis=1)
    live_rows = (row_place < row_limit).astype(jnp.float32)[:, None]
    row_weight = live_rows * jnp.where(row_side % 2 == 0, -1.0, 1.0).astype(jnp.float32)[:, None]
    inverse_map = jnp.argsort(slot_map)
    position = lax.axis_index("sub")
    lower_zeros = jnp.zeros((2 * face_rows, columns), jnp.float32)

    def assemble(values):
        blocks = (values * row_weight).reshape(4, face_rows, columns)
        along_sub = blocks[0:2]
        along_cluster = blocks[2:4]
        sub_halo = extended(along_sub, (("sub", 0),), 1)
        cluster_halo = extended(along_cluster, (("cluster", 0),), 1)
        joined = jnp.concatenate(
            [join_pair(along_sub, sub_halo), join_pair(along_cluster, cluster_halo)], axis=0
        )
        return joined.reshape(orders, columns) * live_rows

    selected = lax.dynamic_slice_in_dim(coarse_matrix, position * mode_count, mode_count, 0)

    def accumulate(piece_rows):
        return matmul(selected, piece_rows)

    def project(values):
        signed = (values * row_weight)[: 2 * face_rows]
        moments = matmul(basis_rows, signed)
        coefficients = accumulate(lax.all_gather(moments, "sub", axis=0, tiled=True))
        lifted = products(basis_rows, coefficients) * row_weight[: 2 * face_rows]
        side_pair = lifted.reshape(2, face_rows, columns)
        coarse_halo = extended(side_pair, (("sub", 0),), 1)
        upper = join_pair(side_pair, coarse_halo).reshape(2 * face_rows, columns)
        correction = jnp.concatenate([upper, lower_zeros], axis=0) * live_rows
        return values - correction

    residual = project(assemble(local_rhs))
    solution = jnp.zeros_like(residual)
    direction = residual
    for iteration in range(ITERS):
        local_vals = jnp.take(project(direction) * row_weight, slot_map, axis=0)
        mapped = matmul(operator, local_vals)
        mapped = project(assemble(jnp.take(mapped, inverse_map, axis=0)))
        curvature, descent = lax.psum(
            (0.5 * products(direction, mapped), 0.5 * products(direction, residual)),
            ("cluster", "sub"),
        )
        factor = jnp.linalg.cholesky(curvature)
        step_size = chol_solve(factor, descent)
        solution = solution + matmul(direction, step_size)
        residual = residual - matmul(mapped, step_size)
        if iteration + 1 < ITERS:
            coupling = lax.psum(0.5 * products(mapped, residual), ("cluster", "sub"))
            direction_mix = -chol_solve(factor, coupling)
            direction = residual + matmul(direction, direction_mix)
    return (solution[None, None], residual[None, None])


def solution(mesh):
    return jax.shard_map(
        shards,
        mesh=mesh,
        in_specs=(
            P("cluster", "sub", None, None),
            P("cluster", "sub", None, None),
            P("cluster", "sub", None),
            P("cluster", "sub", None),
            P("cluster", "sub", None, None),
            P("cluster", None, None),
        ),
        out_specs=(P("cluster", "sub", None, None), P("cluster", "sub", None, None)),
        check_vma=False,
    )
```

profile of v0, /device:TPU:1, one launch (start us, length us, event | category | flops | bytes accessed | tf_op | source)
XLA Modules:
  0.0 490.3 jit_solution(13150986672781962935)
XLA Ops:
  2.7 4.9 %collective-permute-start = (f32[1,352,64]{1,2,0:T(8,128)S(1)}, f32[1,352,64]{1,2,0:T(8,128)S(1)}, u32[]{:S(2)}, u32[]{:S(2)}) collective-permute-start(f32[1,352,64]{1,2,0:T(8,128)S(1)} %get-tuple-element.34), channel_id=1, source_target_pairs={{0,1},{1,2},{2,3},{3,4},{4,5},{5,6},{6,7},{7,8},{8,9},{9,10},{10,1... | collective-permute-start | bytes 270344 | tf_op jit(solution)/shard_map/ppermute | solution.py:17
  7.6 3.2 collective-permute-start.2
  10.9 1.3 collective-permute-start.3
  12.2 1.9 collective-permute-start.1
  14.9 5.0 %sort.17 = (s32[1408]{0:T(1024)}, s32[1408]{0:T(1024)S(1)}) sort(s32[1408]{0:T(1024)S(1)} %reduce.5, s32[1408]{0:T(1024)S(1)} %iota.76), dimensions={0}, to_apply=%region_1.3 | sort | flops 15488 | bytes 22528 | tf_op jit(solution)/shard_map/jit(argsort)/sort | solution.py:60
  22.0 20.7 %all_gather.15 = f32[512,64]{1,0:T(8,128)S(1)} all-gather(f32[32,64]{1,0:T(8,128)S(1)} %convolution_bitcast_fusion.4), channel_id=1, replica_groups=mesh['cluster'=16,'sub'=16] {'sub'}, dimensions={0}, use_global_device_ids=true | all-gather | bytes 139264 | tf_op jit(solution)/shard_map/all_gather | solution.py:83
  44.3 1.9 collective-permute-start.4
  46.2 2.4 collective-permute-start.5
  48.7 3.5 collective-permute-done.5
  53.0 15.7 %all_gather.16 = f32[512,64]{1,0:T(8,128)S(1)} all-gather(f32[32,64]{1,0:T(8,128)S(1)} %convolution_bitcast_fusion.3), channel_id=1, replica_groups=mesh['cluster'=16,'sub'=16] {'sub'}, dimensions={0}, use_global_device_ids=true | all-gather | bytes 139264 | tf_op jit(solution)/shard_map/all_gather | solution.py:83
  69.4 1.9 collective-permute-start.6
  71.4 2.4 collective-permute-start.7
  73.8 3.5 collective-permute-done.7
  78.1 2.7 gather_fusion
  80.8 10.9 %fusion.6 = f32[1408,64]{0,1:T(8,128)S(1)} fusion(f32[1,1,1408,1408]{3,2,1,0:T(8,128)} %param.13, f32[1408,64]{1,0:T(8,128)S(1)} %gather_fusion, pred[1408]{0:T(1024)(128)(4,1)S(1)} %compare_and_fusion.1), kind=kOutput, calls=%fused_computation.14 | convolution fusion | flops 1522622464 | bytes 8652160 | tf_op jit(solution)/shard_map/dot_general | solution.py:30
  91.9 2.7 gather_fusion.1
  95.1 1.9 collective-permute-start.8
  97.0 4.0 collective-permute-start.10
  102.3 2.7 collective-permute-start.9
  105.0 1.3 collective-permute-done.11
  106.3 1.9 collective-permute-done.9
  109.2 18.1 %all_gather.17 = f32[512,64]{1,0:T(8,128)S(1)} all-gather(f32[32,64]{1,0:T(8,128)S(1)} %convolution_bitcast_fusion.2), channel_id=1, replica_groups=mesh['cluster'=16,'sub'=16] {'sub'}, dimensions={0}, use_global_device_ids=true | all-gather | bytes 139264 | tf_op jit(solution)/shard_map/all_gather | solution.py:83
  128.0 2.2 collective-permute-start.12
  130.2 2.3 collective-permute-start.13
  133.0 3.1 collective-permute-done.13
  137.1 82.8 %all-reduce.6 = (f32[64,64]{0,1:T(8,128)S(1)}, f32[64,64]{0,1:T(8,128)S(1)}) all-reduce(f32[64,64]{0,1:T(8,128)S(1)} %convolution_multiply_fusion.8, f32[64,64]{0,1:T(8,128)S(1)} %convolution_multiply_fusion.9), channel_id=1, replica_groups=mesh['cluster'=16,'sub'=16] {'cluster','sub'}, use_global_device_ids=true, to_apply=%region_5.8 | all-reduce | flops 8192 | bytes 65536 | tf_op jit(solution)/shard_map/psum | solution.py:98
  220.0 5.8 %cholesky.44 = f32[64,64]{1,0:T(8,128)S(1)} custom-call(f32[64,64]{1,0:T(8,128)S(1)} %fusion.69), custom_call_target="Cholesky" | custom-call | tf_op jit(solution)/shard_map/jit(cholesky)/cholesky | solution.py:102
  227.2 4.9 custom-call.13
  233.5 72.9 %psum.37 = f32[64,64]{0,1:T(8,128)S(1)} all-reduce(f32[64,64]{0,1:T(8,128)S(1)} %convolution_multiply_fusion.7), channel_id=1, replica_groups=mesh['cluster'=16,'sub'=16] {'cluster','sub'}, use_global_device_ids=true, to_apply=%region_6.11 | all-reduce | flops 4096 | bytes 32768 | tf_op jit(solution)/shard_map/psum | solution.py:107
  307.6 17.4 %all_gather.18 = f32[512,64]{1,0:T(8,128)S(1)} all-gather(f32[32,64]{1,0:T(8,128)S(1)} %convolution_bitcast_fusion.1), channel_id=1, replica_groups=mesh['cluster'=16,'sub'=16] {'sub'}, dimensions={0}, use_global_device_ids=true | all-gather | bytes 139264 | tf_op jit(solution)/shard_map/all_gather | solution.py:83
  325.8 1.9 collective-permute-start.14
  327.7 2.6 collective-permute-start.15
  330.3 3.3 collective-permute-done.15
  334.4 3.6 gather_fusion.2
  338.1 11.0 %fusion.9 = f32[1408,64]{0,1:T(8,128)S(1)} fusion(f32[1,1,1408,1408]{3,2,1,0:T(8,128)} %param.13, f32[1408,64]{1,0:T(8,128)} %gather_fusion.2, pred[1408]{0:T(1024)(128)(4,1)S(1)} %compare_and_fusion.1), kind=kOutput, calls=%fused_computation.15 | convolution fusion | flops 1522622464 | bytes 8652160 | tf_op jit(solution)/shard_map/dot_general | solution.py:30
  349.4 3.6 gather_fusion.3
  353.0 1.4 copy.75
  354.6 1.9 collective-permute-start.16
  356.5 2.9 collective-permute-start.18
  360.7 2.7 collective-permute-start.17
  364.7 1.9 collective-permute-done.17
  367.6 17.8 %all_gather.19 = f32[512,64]{1,0:T(8,128)S(1)} all-gather(f32[32,64]{1,0:T(8,128)S(1)} %convolution_bitcast_fusion), channel_id=1, replica_groups=mesh['cluster'=16,'sub'=16] {'sub'}, dimensions={0}, use_global_device_ids=true | all-gather | bytes 139264 | tf_op jit(solution)/shard_map/all_gather | solution.py:83
  386.1 2.1 collective-permute-start.20
  388.2 2.2 collective-permute-start.21
  391.0 3.2 collective-permute-done.21
  395.1 80.1 %all-reduce.5 = (f32[64,64]{0,1:T(8,128)S(1)}, f32[64,64]{0,1:T(8,128)S(1)}) all-reduce(f32[64,64]{0,1:T(8,128)S(1)} %convolution_multiply_fusion.5, f32[64,64]{0,1:T(8,128)S(1)} %convolution_multiply_fusion.6), channel_id=1, replica_groups=mesh['cluster'=16,'sub'=16] {'cluster','sub'}, use_global_device_ids=true, to_apply=%region_8.13 | all-reduce | flops 8192 | bytes 65536 | tf_op jit(solution)/shard_map/psum | solution.py:98
  475.3 5.8 %cholesky.55 = f32[64,64]{1,0:T(8,128)S(1)} custom-call(f32[64,64]{1,0:T(8,128)S(1)} %fusion.61), custom_call_target="Cholesky" | custom-call | tf_op jit(solution)/shard_map/jit(cholesky)/cholesky | solution.py:102
  482.5 4.9 custom-call.17
  (132 shorter events, 29.6 us)
Async XLA Ops:
  0.6 42.1 %copy-start = (f32[1,512,512]{2,1,0:T(8,128)S(1)}, f32[1,512,512]{2,1,0:T(8,128)}, u32[]{:S(2)}) copy-start(f32[1,512,512]{2,1,0:T(8,128)} %param.18) | copy-start | bytes 3145732
  0.6 52.0 %copy-start.1 = (f32[1,1,32,704]{3,2,1,0:T(8,128)S(1)}, f32[1,1,32,704]{3,2,1,0:T(8,128)}, u32[]{:S(2)}) copy-start(f32[1,1,32,704]{3,2,1,0:T(8,128)} %param.17) | copy-start | bytes 270340
  2.7 17.3 %collective-permute-start = (f32[1,352,64]{1,2,0:T(8,128)S(1)}, f32[1,352,64]{1,2,0:T(8,128)S(1)}, u32[]{:S(2)}, u32[]{:S(2)}) collective-permute-start(f32[1,352,64]{1,2,0:T(8,128)S(1)} %get-tuple-element.34), channel_id=1, source_target_pairs={{0,1},{1,2},{2,3},{3,4},{4,5},{5,6},{6,7},{7,8},{8,9},{9,10},{10,1... | collective-permute-start | bytes 270344 | tf_op jit(solution)/shard_map/ppermute | solution.py:17
  7.6 12.4 %collective-permute-start.2 = (f32[1,352,64]{1,2,0:T(8,128)S(1)}, f32[1,352,64]{1,2,0:T(8,128)S(1)}, u32[]{:S(2)}, u32[]{:S(2)}) collective-permute-start(f32[1,352,64]{1,2,0:T(8,128)S(1)} %get-tuple-element.35), channel_id=1, source_target_pairs={{0,16},{16,32},{32,48},{48,64},{64,80},{80,96},{96,112},{112,128},... | collective-permute-start | bytes 270344 | tf_op jit(solution)/shard_map/ppermute | solution.py:17
  10.9 9.2 %collective-permute-start.3 = (f32[1,352,64]{1,2,0:T(8,128)S(1)}, f32[1,352,64]{1,2,0:T(8,128)S(1)}, u32[]{:S(2)}, u32[]{:S(2)}) collective-permute-start(f32[1,352,64]{1,2,0:T(8,128)S(1)} %get-tuple-element.36), channel_id=1, source_target_pairs={{16,0},{32,16},{48,32},{64,48},{80,64},{96,80},{112,96},{128,112},... | collective-permute-start | bytes 270344 | tf_op jit(solution)/shard_map/ppermute | solution.py:18
  12.2 7.9 %collective-permute-start.1 = (f32[1,352,64]{1,2,0:T(8,128)S(1)}, f32[1,352,64]{1,2,0:T(8,128)S(1)}, u32[]{:S(2)}, u32[]{:S(2)}) collective-permute-start(f32[1,352,64]{1,2,0:T(8,128)S(1)} %get-tuple-element.37), channel_id=1, source_target_pairs={{1,0},{2,1},{3,2},{4,3},{5,4},{6,5},{7,6},{8,7},{9,8},{10,9},{11,1... | collective-permute-start | bytes 270344 | tf_op jit(solution)/shard_map/ppermute | solution.py:18
  44.3 4.4 collective-permute-start.4
  46.2 5.9 %collective-permute-start.5 = (f32[1,352,64]{1,2,0:T(8,128)S(1)}, f32[1,352,64]{1,2,0:T(8,128)S(1)}, u32[]{:S(2)}, u32[]{:S(2)}) collective-permute-start(f32[1,352,64]{1,2,0:T(8,128)S(1)} %get-tuple-element.57), channel_id=1, source_target_pairs={{1,0},{2,1},{3,2},{4,3},{5,4},{6,5},{7,6},{8,7},{9,8},{10,9},{11,1... | collective-permute-start | bytes 270344 | tf_op jit(solution)/shard_map/ppermute | solution.py:18
  69.4 4.4 collective-permute-start.6
  71.4 5.9 %collective-permute-start.7 = (f32[1,352,64]{1,2,0:T(8,128)S(1)}, f32[1,352,64]{1,2,0:T(8,128)S(1)}, u32[]{:S(2)}, u32[]{:S(2)}) collective-permute-start(f32[1,352,64]{1,2,0:T(8,128)S(1)} %get-tuple-element.53), channel_id=1, source_target_pairs={{1,0},{2,1},{3,2},{4,3},{5,4},{6,5},{7,6},{8,7},{9,8},{10,9},{11,1... | collective-permute-start | bytes 270344 | tf_op jit(solution)/shard_map/ppermute | solution.py:18
  95.1 9.9 %collective-permute-start.8 = (f32[1,352,64]{1,2,0:T(8,128)S(1)}, f32[1,352,64]{1,2,0:T(8,128)S(1)}, u32[]{:S(2)}, u32[]{:S(2)}) collective-permute-start(f32[1,352,64]{1,2,0:T(8,128)S(1)} %get-tuple-element.26), channel_id=1, source_target_pairs={{0,1},{1,2},{2,3},{3,4},{4,5},{5,6},{6,7},{7,8},{8,9},{9,10},{10,1... | collective-permute-start | bytes 270344 | tf_op jit(solution)/shard_map/ppermute | solution.py:17
  97.0 8.0 %collective-permute-start.10 = (f32[1,352,64]{1,2,0:T(8,128)S(1)}, f32[1,352,64]{1,2,0:T(8,128)S(1)}, u32[]{:S(2)}, u32[]{:S(2)}) collective-permute-start(f32[1,352,64]{1,2,0:T(8,128)S(1)} %get-tuple-element.27), channel_id=1, source_target_pairs={{0,16},{16,32},{32,48},{48,64},{64,80},{80,96},{96,112},{112,128},... | collective-permute-start | bytes 270344 | tf_op jit(solution)/shard_map/ppermute | solution.py:17
  101.0 5.4 %collective-permute-start.11 = (f32[1,352,64]{1,2,0:T(8,128)S(1)}, f32[1,352,64]{1,2,0:T(8,128)S(1)}, u32[]{:S(2)}, u32[]{:S(2)}) collective-permute-start(f32[1,352,64]{1,2,0:T(8,128)S(1)} %get-tuple-element.28), channel_id=1, source_target_pairs={{16,0},{32,16},{48,32},{64,48},{80,64},{96,80},{112,96},{128,112},... | collective-permute-start | bytes 270344 | tf_op jit(solution)/shard_map/ppermute | solution.py:18
  102.3 5.9 %collective-permute-start.9 = (f32[1,352,64]{1,2,0:T(8,128)S(1)}, f32[1,352,64]{1,2,0:T(8,128)S(1)}, u32[]{:S(2)}, u32[]{:S(2)}) collective-permute-start(f32[1,352,64]{1,2,0:T(8,128)S(1)} %get-tuple-element.29), channel_id=1, source_target_pairs={{1,0},{2,1},{3,2},{4,3},{5,4},{6,5},{7,6},{8,7},{9,8},{10,9},{11,1... | collective-permute-start | bytes 270344 | tf_op jit(solution)/shard_map/ppermute | solution.py:18
  128.0 5.0 %collective-permute-start.12 = (f32[1,352,64]{1,2,0:T(8,128)S(1)}, f32[1,352,64]{1,2,0:T(8,128)S(1)}, u32[]{:S(2)}, u32[]{:S(2)}) collective-permute-start(f32[1,352,64]{1,2,0:T(8,128)S(1)} %get-tuple-element.48), channel_id=1, source_target_pairs={{0,1},{1,2},{2,3},{3,4},{4,5},{5,6},{6,7},{7,8},{8,9},{9,10},{10,1... | collective-permute-start | bytes 270344 | tf_op jit(solution)/shard_map/ppermute | solution.py:17
  130.2 5.9 %collective-permute-start.13 = (f32[1,352,64]{1,2,0:T(8,128)S(1)}, f32[1,352,64]{1,2,0:T(8,128)S(1)}, u32[]{:S(2)}, u32[]{:S(2)}) collective-permute-start(f32[1,352,64]{1,2,0:T(8,128)S(1)} %get-tuple-element.49), channel_id=1, source_target_pairs={{1,0},{2,1},{3,2},{4,3},{5,4},{6,5},{7,6},{8,7},{9,8},{10,9},{11,1... | collective-permute-start | bytes 270344 | tf_op jit(solution)/shard_map/ppermute | solution.py:18
  325.8 4.6 collective-permute-start.14
  327.7 5.9 %collective-permute-start.15 = (f32[1,352,64]{1,2,0:T(8,128)S(1)}, f32[1,352,64]{1,2,0:T(8,128)S(1)}, u32[]{:S(2)}, u32[]{:S(2)}) collective-permute-start(f32[1,352,64]{1,2,0:T(8,128)S(1)} %get-tuple-element.45), channel_id=1, source_target_pairs={{1,0},{2,1},{3,2},{4,3},{5,4},{6,5},{7,6},{8,7},{9,8},{10,9},{11,1... | collective-permute-start | bytes 270344 | tf_op jit(solution)/shard_map/ppermute | solution.py:18
  354.6 9.3 %collective-permute-start.16 = (f32[1,352,64]{1,2,0:T(8,128)S(1)}, f32[1,352,64]{1,2,0:T(8,128)S(1)}, u32[]{:S(2)}, u32[]{:S(2)}) collective-permute-start(f32[1,352,64]{1,2,0:T(8,128)S(1)} %get-tuple-element.18), channel_id=1, source_target_pairs={{0,1},{1,2},{2,3},{3,4},{4,5},{5,6},{6,7},{7,8},{8,9},{9,10},{10,1... | collective-permute-start | bytes 270344 | tf_op jit(solution)/shard_map/ppermute | solution.py:17
  356.5 7.4 %collective-permute-start.18 = (f32[1,352,64]{1,2,0:T(8,128)S(1)}, f32[1,352,64]{1,2,0:T(8,128)S(1)}, u32[]{:S(2)}, u32[]{:S(2)}) collective-permute-start(f32[1,352,64]{1,2,0:T(8,128)S(1)} %get-tuple-element.19), channel_id=1, source_target_pairs={{0,16},{16,32},{32,48},{48,64},{64,80},{80,96},{96,112},{112,128},... | collective-permute-start | bytes 270344 | tf_op jit(solution)/shard_map/ppermute | solution.py:17
  359.4 5.4 %collective-permute-start.19 = (f32[1,352,64]{1,2,0:T(8,128)S(1)}, f32[1,352,64]{1,2,0:T(8,128)S(1)}, u32[]{:S(2)}, u32[]{:S(2)}) collective-permute-start(f32[1,352,64]{1,2,0:T(8,128)S(1)} %get-tuple-element.20), channel_id=1, source_target_pairs={{16,0},{32,16},{48,32},{64,48},{80,64},{96,80},{112,96},{128,112},... | collective-permute-start | bytes 270344 | tf_op jit(solution)/shard_map/ppermute | solution.py:18
  360.7 5.9 %collective-permute-start.17 = (f32[1,352,64]{1,2,0:T(8,128)S(1)}, f32[1,352,64]{1,2,0:T(8,128)S(1)}, u32[]{:S(2)}, u32[]{:S(2)}) collective-permute-start(f32[1,352,64]{1,2,0:T(8,128)S(1)} %get-tuple-element.21), channel_id=1, source_target_pairs={{1,0},{2,1},{3,2},{4,3},{5,4},{6,5},{7,6},{8,7},{9,8},{10,9},{11,1... | collective-permute-start | bytes 270344 | tf_op jit(solution)/shard_map/ppermute | solution.py:18
  386.1 4.8 collective-permute-start.20
  388.2 5.9 %collective-permute-start.21 = (f32[1,352,64]{1,2,0:T(8,128)S(1)}, f32[1,352,64]{1,2,0:T(8,128)S(1)}, u32[]{:S(2)}, u32[]{:S(2)}) collective-permute-start(f32[1,352,64]{1,2,0:T(8,128)S(1)} %get-tuple-element.41), channel_id=1, source_target_pairs={{1,0},{2,1},{3,2},{4,3},{5,4},{6,5},{7,6},{8,7},{9,8},{10,9},{11,1... | collective-permute-start | bytes 270344 | tf_op jit(solution)/shard_map/ppermute | solution.py:18
where the time goes:
time: 492 us; the launch traced here: 490 us
  blocking collectives  326 us (66%)
  starting transfers between devices  52 us (11%)
  matrix products  35.9 us (7%)
  other arithmetic  33.3 us (7%)
  waiting for transfers between devices  22.5 us (5%)
  local copies, waits for them, and re-layouts  19.4 us (4%)
    psum x2, blocking collectives, shards(): lax.psum((0.5 * products(direction, mapped), 0.5 * products(direction, re...  163 us
    all_gather x5, blocking collectives, project(): lax.all_gather(moments, 'sub', axis=0, tiled=True)  89.7 us
    psum x1, blocking collectives, shards(): coupling = lax.psum(0.5 * products(mapped, residual), ('cluster', 'sub'))  72.9 us
    dot_general x17, matrix products, matmul(): jnp.dot(left, right, precision=precise, preferred_element_type=jnp.float32)  29.5 us
    ppermute x11, starting transfers between devices, extended(): before = lax.ppermute(last, axis, up)  28.8 us
    ppermute x11, starting transfers between devices, extended(): after = lax.ppermute(leading, axis, down)  23.2 us
    ppermute x11, waiting for transfers between devices, extended(): after = lax.ppermute(leading, axis, down)  22.5 us
    another operation x6, other arithmetic, shards(): factor = jnp.linalg.cholesky(curvature)  13 us
  transfers between devices with their start and end apart: 22, of which 9 were waited for; matrix products, arithmetic and copies ran while one was open for 1% of the time, Pallas kernels for 0%

commit v1 on v0

--- a/solution.py
+++ b/solution.py
@@ -96,8 +96,10 @@
         mapped = matmul(operator, local_vals)
         mapped = project(assemble(jnp.take(mapped, inverse_map, axis=0)))
         curvature, descent = lax.psum(
-            (0.5 * products(direction, mapped), 0.5 * products(direction, residual)),
-            ("cluster", "sub"),
+            lax.psum(
+                (0.5 * products(direction, mapped), 0.5 * products(direction, residual)), "cluster"
+            ),
+            "sub",
         )
         factor = jnp.linalg.cholesky(curvature)
         step_size = chol_solve(factor, descent)

time: 492 us -> 564 us (1.15)
  blocking collectives: 326 us -> 396 us
    psum x0 -> x2, blocking collectives: none -> 110 us  [shards(): lax.psum(lax.psum((0.5 * products(direction, mapped), 0.5 * products(dire...]
    psum x2, blocking collectives: 163 us -> 120 us  [shards(): lax.psum((0.5 * products(direction, mapped), 0.5 * products(direction, re...]
where the time goes in v1:
time: 564 us; the launch traced here: 561 us
  blocking collectives  396 us (70%)
  starting transfers between devices  52.3 us (9%)
  matrix products  35.9 us (6%)
  other arithmetic  33.3 us (6%)
  waiting for transfers between devices  22.6 us (4%)
  local copies, waits for them, and re-layouts  19.4 us (3%)
    psum x2, blocking collectives, shards(): lax.psum((0.5 * products(direction, mapped), 0.5 * products(direction, re...  120 us
    psum x2, blocking collectives, shards(): lax.psum(lax.psum((0.5 * products(direction, mapped), 0.5 * products(dire...  110 us
    all_gather x5, blocking collectives, project(): lax.all_gather(moments, 'sub', axis=0, tiled=True)  89.4 us
    psum x1, blocking collectives, shards(): coupling = lax.psum(0.5 * products(mapped, residual), ('cluster', 'sub'))  77.3 us
    dot_general x17, matrix products, matmul(): jnp.dot(left, right, precision=precise, preferred_element_type=jnp.float32)  29.5 us
    ppermute x11, starting transfers between devices, extended(): before = lax.ppermute(last, axis, up)  29.2 us
    ppermute x11, starting transfers between devices, extended(): after = lax.ppermute(leading, axis, down)  23.2 us
    ppermute x11, waiting for transfers between devices, extended(): after = lax.ppermute(leading, axis, down)  22.6 us
  transfers between devices with their start and end apart: 22, of which 9 were waited for; matrix products, arithmetic and copies ran while one was open for 1% of the time, Pallas kernels for 0%

profile of v1, /device:TPU:1, one launch (start us, length us, event | category | flops | bytes accessed | tf_op | source)
XLA Modules:
  0.0 561.2 jit_solution(9594386711244053501)
XLA Ops:
  2.7 4.9 collective-permute-start
  7.6 3.2 collective-permute-start.2
  12.2 1.9 collective-permute-start.1
  14.9 5.0 sort.17
  22.0 20.7 %all_gather.15 = f32[512,64]{1,0:T(8,128)S(1)} all-gather(f32[32,64]{1,0:T(8,128)S(1)} %convolution_bitcast_fusion.4), channel_id=1, replica_groups=mesh['cluster'=16,'sub'=16] {'sub'}, dimensions={0}, use_global_device_ids=true | all-gather | bytes 139264 | tf_op jit(solution)/shard_map/all_gather | solution.py:83
  44.3 1.9 collective-permute-start.4
  46.2 2.4 collective-permute-start.5
  48.7 3.5 collective-permute-done.5
  53.0 15.7 %all_gather.16 = f32[512,64]{1,0:T(8,128)S(1)} all-gather(f32[32,64]{1,0:T(8,128)S(1)} %convolution_bitcast_fusion.3), channel_id=1, replica_groups=mesh['cluster'=16,'sub'=16] {'sub'}, dimensions={0}, use_global_device_ids=true | all-gather | bytes 139264 | tf_op jit(solution)/shard_map/all_gather | solution.py:83
  69.4 1.9 collective-permute-start.6
  71.4 2.4 collective-permute-start.7
  73.8 3.5 collective-permute-done.7
  78.1 2.7 gather_fusion
  80.8 10.9 %fusion.6 = f32[1408,64]{0,1:T(8,128)S(1)} fusion(f32[1,1,1408,1408]{3,2,1,0:T(8,128)} %param.13, f32[1408,64]{1,0:T(8,128)S(1)} %gather_fusion, pred[1408]{0:T(1024)(128)(4,1)S(1)} %compare_and_fusion.1), kind=kOutput, calls=%fused_computation.14 | convolution fusion | flops 1522622464 | bytes 8652160 | tf_op jit(solution)/shard_map/dot_general | solution.py:30
  91.9 2.7 gather_fusion.1
  95.1 1.9 collective-permute-start.8
  97.0 4.0 collective-permute-start.10
  102.3 2.7 collective-permute-start.9
  106.3 1.9 collective-permute-done.9
  109.2 18.1 %all_gather.17 = f32[512,64]{1,0:T(8,128)S(1)} all-gather(f32[32,64]{1,0:T(8,128)S(1)} %convolution_bitcast_fusion.2), channel_id=1, replica_groups=mesh['cluster'=16,'sub'=16] {'sub'}, dimensions={0}, use_global_device_ids=true | all-gather | bytes 139264 | tf_op jit(solution)/shard_map/all_gather | solution.py:83
  128.0 2.2 collective-permute-start.12
  130.2 2.3 collective-permute-start.13
  133.0 3.1 collective-permute-done.13
  137.1 61.3 %all-reduce.8 = (f32[64,64]{0,1:T(8,128)S(1)}, f32[64,64]{0,1:T(8,128)S(1)}) all-reduce(f32[64,64]{0,1:T(8,128)S(1)} %convolution_multiply_fusion.8, f32[64,64]{0,1:T(8,128)S(1)} %convolution_multiply_fusion.9), channel_id=1, replica_groups=mesh['cluster'=16,'sub'=16] {'cluster'}, use_global_device_ids=true, to_apply=%region_6.9 | all-reduce | flops 8192 | bytes 65536 | tf_op jit(solution)/shard_map/psum | solution.py:99
  198.4 55.0 %all-reduce.6 = (f32[64,64]{0,1:T(8,128)S(1)}, f32[64,64]{0,1:T(8,128)S(1)}) all-reduce(f32[64,64]{0,1:T(8,128)S(1)} %get-tuple-element.14, f32[64,64]{0,1:T(8,128)S(1)} %get-tuple-element.15), channel_id=1, replica_groups=mesh['cluster'=16,'sub'=16] {'sub'}, use_global_device_ids=true, to_apply=%region_7.10 | all-reduce | flops 8192 | bytes 65536 | tf_op jit(solution)/shard_map/psum | solution.py:98
  253.5 5.8 %cholesky.44 = f32[64,64]{1,0:T(8,128)S(1)} custom-call(f32[64,64]{1,0:T(8,128)S(1)} %fusion.69), custom_call_target="Cholesky" | custom-call | tf_op jit(solution)/shard_map/jit(cholesky)/cholesky | solution.py:104
  260.7 4.9 custom-call.13
  267.0 77.3 %psum.67 = f32[64,64]{0,1:T(8,128)S(1)} all-reduce(f32[64,64]{0,1:T(8,128)S(1)} %convolution_multiply_fusion.7), channel_id=1, replica_groups=mesh['cluster'=16,'sub'=16] {'cluster','sub'}, use_global_device_ids=true, to_apply=%region_8.13 | all-reduce | flops 4096 | bytes 32768 | tf_op jit(solution)/shard_map/psum | solution.py:109
  345.6 17.1 %all_gather.18 = f32[512,64]{1,0:T(8,128)S(1)} all-gather(f32[32,64]{1,0:T(8,128)S(1)} %convolution_bitcast_fusion.1), channel_id=1, replica_groups=mesh['cluster'=16,'sub'=16] {'sub'}, dimensions={0}, use_global_device_ids=true | all-gather | bytes 139264 | tf_op jit(solution)/shard_map/all_gather | solution.py:83
  363.4 2.0 collective-permute-start.14
  365.3 2.6 collective-permute-start.15
  367.9 3.3 collective-permute-done.15
  372.0 3.7 gather_fusion.2
  375.7 11.0 %fusion.9 = f32[1408,64]{0,1:T(8,128)S(1)} fusion(f32[1,1,1408,1408]{3,2,1,0:T(8,128)} %param.13, f32[1408,64]{1,0:T(8,128)} %gather_fusion.2, pred[1408]{0:T(1024)(128)(4,1)S(1)} %compare_and_fusion.1), kind=kOutput, calls=%fused_computation.15 | convolution fusion | flops 1522622464 | bytes 8652160 | tf_op jit(solution)/shard_map/dot_general | solution.py:30
  387.0 3.7 gather_fusion.3
  390.7 1.4 copy.75
  392.2 1.9 collective-permute-start.16
  394.2 3.2 collective-permute-start.18
  398.6 2.7 collective-permute-start.17
  402.7 1.9 collective-permute-done.17
  405.6 17.8 %all_gather.19 = f32[512,64]{1,0:T(8,128)S(1)} all-gather(f32[32,64]{1,0:T(8,128)S(1)} %convolution_bitcast_fusion), channel_id=1, replica_groups=mesh['cluster'=16,'sub'=16] {'sub'}, dimensions={0}, use_global_device_ids=true | all-gather | bytes 139264 | tf_op jit(solution)/shard_map/all_gather | solution.py:83
  424.1 2.1 collective-permute-start.20
  426.2 2.2 collective-permute-start.21
  428.9 3.2 collective-permute-done.21
  433.1 58.5 %all-reduce.7 = (f32[64,64]{0,1:T(8,128)S(1)}, f32[64,64]{0,1:T(8,128)S(1)}) all-reduce(f32[64,64]{0,1:T(8,128)S(1)} %convolution_multiply_fusion.5, f32[64,64]{0,1:T(8,128)S(1)} %convolution_multiply_fusion.6), channel_id=1, replica_groups=mesh['cluster'=16,'sub'=16] {'cluster'}, use_global_device_ids=true, to_apply=%region_11.16 | all-reduce | flops 8192 | bytes 65536 | tf_op jit(solution)/shard_map/psum | solution.py:99
  491.5 54.6 %all-reduce.5 = (f32[64,64]{0,1:T(8,128)S(1)}, f32[64,64]{0,1:T(8,128)S(1)}) all-reduce(f32[64,64]{0,1:T(8,128)S(1)} %get-tuple-element.12, f32[64,64]{0,1:T(8,128)S(1)} %get-tuple-element.13), channel_id=1, replica_groups=mesh['cluster'=16,'sub'=16] {'sub'}, use_global_device_ids=true, to_apply=%region_12.17 | all-reduce | flops 8192 | bytes 65536 | tf_op jit(solution)/shard_map/psum | solution.py:98
  546.2 5.8 %cholesky.55 = f32[64,64]{1,0:T(8,128)S(1)} custom-call(f32[64,64]{1,0:T(8,128)S(1)} %fusion.61), custom_call_target="Cholesky" | custom-call | tf_op jit(solution)/shard_map/jit(cholesky)/cholesky | solution.py:104
  553.4 4.9 custom-call.17
  (134 shorter events, 32.2 us)
Async XLA Ops:
  0.6 42.1 %copy-start = (f32[1,512,512]{2,1,0:T(8,128)S(1)}, f32[1,512,512]{2,1,0:T(8,128)}, u32[]{:S(2)}) copy-start(f32[1,512,512]{2,1,0:T(8,128)} %param.18) | copy-start | bytes 3145732
  0.6 52.0 %copy-start.1 = (f32[1,1,32,704]{3,2,1,0:T(8,128)S(1)}, f32[1,1,32,704]{3,2,1,0:T(8,128)}, u32[]{:S(2)}) copy-start(f32[1,1,32,704]{3,2,1,0:T(8,128)} %param.17) | copy-start | bytes 270340
  2.7 17.3 %collective-permute-start = (f32[1,352,64]{1,2,0:T(8,128)S(1)}, f32[1,352,64]{1,2,0:T(8,128)S(1)}, u32[]{:S(2)}, u32[]{:S(2)}) collective-permute-start(f32[1,352,64]{1,2,0:T(8,128)S(1)} %get-tuple-element.38), channel_id=1, source_target_pairs={{0,1},{1,2},{2,3},{3,4},{4,5},{5,6},{6,7},{7,8},{8,9},{9,10},{10,1... | collective-permute-start | bytes 270344 | tf_op jit(solution)/shard_map/ppermute | solution.py:17
  7.6 12.4 %collective-permute-start.2 = (f32[1,352,64]{1,2,0:T(8,128)S(1)}, f32[1,352,64]{1,2,0:T(8,128)S(1)}, u32[]{:S(2)}, u32[]{:S(2)}) collective-permute-start(f32[1,352,64]{1,2,0:T(8,128)S(1)} %get-tuple-element.39), channel_id=1, source_target_pairs={{0,16},{16,32},{32,48},{48,64},{64,80},{80,96},{96,112},{112,128},... | collective-permute-start | bytes 270344 | tf_op jit(solution)/shard_map/ppermute | solution.py:17
  10.9 9.2 %collective-permute-start.3 = (f32[1,352,64]{1,2,0:T(8,128)S(1)}, f32[1,352,64]{1,2,0:T(8,128)S(1)}, u32[]{:S(2)}, u32[]{:S(2)}) collective-permute-start(f32[1,352,64]{1,2,0:T(8,128)S(1)} %get-tuple-element.40), channel_id=1, source_target_pairs={{16,0},{32,16},{48,32},{64,48},{80,64},{96,80},{112,96},{128,112},... | collective-permute-start | bytes 270344 | tf_op jit(solution)/shard_map/ppermute | solution.py:18
  12.2 7.9 %collective-permute-start.1 = (f32[1,352,64]{1,2,0:T(8,128)S(1)}, f32[1,352,64]{1,2,0:T(8,128)S(1)}, u32[]{:S(2)}, u32[]{:S(2)}) collective-permute-start(f32[1,352,64]{1,2,0:T(8,128)S(1)} %get-tuple-element.41), channel_id=1, source_target_pairs={{1,0},{2,1},{3,2},{4,3},{5,4},{6,5},{7,6},{8,7},{9,8},{10,9},{11,1... | collective-permute-start | bytes 270344 | tf_op jit(solution)/shard_map/ppermute | solution.py:18
  44.3 4.4 collective-permute-start.4
  46.2 5.9 %collective-permute-start.5 = (f32[1,352,64]{1,2,0:T(8,128)S(1)}, f32[1,352,64]{1,2,0:T(8,128)S(1)}, u32[]{:S(2)}, u32[]{:S(2)}) collective-permute-start(f32[1,352,64]{1,2,0:T(8,128)S(1)} %get-tuple-element.61), channel_id=1, source_target_pairs={{1,0},{2,1},{3,2},{4,3},{5,4},{6,5},{7,6},{8,7},{9,8},{10,9},{11,1... | collective-permute-start | bytes 270344 | tf_op jit(solution)/shard_map/ppermute | solution.py:18
  69.4 4.4 collective-permute-start.6
  71.4 5.9 %collective-permute-start.7 = (f32[1,352,64]{1,2,0:T(8,128)S(1)}, f32[1,352,64]{1,2,0:T(8,128)S(1)}, u32[]{:S(2)}, u32[]{:S(2)}) collective-permute-start(f32[1,352,64]{1,2,0:T(8,128)S(1)} %get-tuple-element.57), channel_id=1, source_target_pairs={{1,0},{2,1},{3,2},{4,3},{5,4},{6,5},{7,6},{8,7},{9,8},{10,9},{11,1... | collective-permute-start | bytes 270344 | tf_op jit(solution)/shard_map/ppermute | solution.py:18
  95.1 9.9 %collective-permute-start.8 = (f32[1,352,64]{1,2,0:T(8,128)S(1)}, f32[1,352,64]{1,2,0:T(8,128)S(1)}, u32[]{:S(2)}, u32[]{:S(2)}) collective-permute-start(f32[1,352,64]{1,2,0:T(8,128)S(1)} %get-tuple-element.30), channel_id=1, source_target_pairs={{0,1},{1,2},{2,3},{3,4},{4,5},{5,6},{6,7},{7,8},{8,9},{9,10},{10,1... | collective-permute-start | bytes 270344 | tf_op jit(solution)/shard_map/ppermute | solution.py:17
  97.0 8.0 %collective-permute-start.10 = (f32[1,352,64]{1,2,0:T(8,128)S(1)}, f32[1,352,64]{1,2,0:T(8,128)S(1)}, u32[]{:S(2)}, u32[]{:S(2)}) collective-permute-start(f32[1,352,64]{1,2,0:T(8,128)S(1)} %get-tuple-element.31), channel_id=1, source_target_pairs={{0,16},{16,32},{32,48},{48,64},{64,80},{80,96},{96,112},{112,128},... | collective-permute-start | bytes 270344 | tf_op jit(solution)/shard_map/ppermute | solution.py:17
  101.0 5.4 collective-permute-start.11
  102.3 5.9 %collective-permute-start.9 = (f32[1,352,64]{1,2,0:T(8,128)S(1)}, f32[1,352,64]{1,2,0:T(8,128)S(1)}, u32[]{:S(2)}, u32[]{:S(2)}) collective-permute-start(f32[1,352,64]{1,2,0:T(8,128)S(1)} %get-tuple-element.33), channel_id=1, source_target_pairs={{1,0},{2,1},{3,2},{4,3},{5,4},{6,5},{7,6},{8,7},{9,8},{10,9},{11,1... | collective-permute-start | bytes 270344 | tf_op jit(solution)/shard_map/ppermute | solution.py:18
  128.0 5.0 collective-permute-start.12
  130.2 5.9 %collective-permute-start.13 = (f32[1,352,64]{1,2,0:T(8,128)S(1)}, f32[1,352,64]{1,2,0:T(8,128)S(1)}, u32[]{:S(2)}, u32[]{:S(2)}) collective-permute-start(f32[1,352,64]{1,2,0:T(8,128)S(1)} %get-tuple-element.53), channel_id=1, source_target_pairs={{1,0},{2,1},{3,2},{4,3},{5,4},{6,5},{7,6},{8,7},{9,8},{10,9},{11,1... | collective-permute-start | bytes 270344 | tf_op jit(solution)/shard_map/ppermute | solution.py:18
  363.4 4.6 collective-permute-start.14
  365.3 5.9 %collective-permute-start.15 = (f32[1,352,64]{1,2,0:T(8,128)S(1)}, f32[1,352,64]{1,2,0:T(8,128)S(1)}, u32[]{:S(2)}, u32[]{:S(2)}) collective-permute-start(f32[1,352,64]{1,2,0:T(8,128)S(1)} %get-tuple-element.49), channel_id=1, source_target_pairs={{1,0},{2,1},{3,2},{4,3},{5,4},{6,5},{7,6},{8,7},{9,8},{10,9},{11,1... | collective-permute-start | bytes 270344 | tf_op jit(solution)/shard_map/ppermute | solution.py:18
  392.2 9.6 %collective-permute-start.16 = (f32[1,352,64]{1,2,0:T(8,128)S(1)}, f32[1,352,64]{1,2,0:T(8,128)S(1)}, u32[]{:S(2)}, u32[]{:S(2)}) collective-permute-start(f32[1,352,64]{1,2,0:T(8,128)S(1)} %get-tuple-element.22), channel_id=1, source_target_pairs={{0,1},{1,2},{2,3},{3,4},{4,5},{5,6},{6,7},{7,8},{8,9},{9,10},{10,1... | collective-permute-start | bytes 270344 | tf_op jit(solution)/shard_map/ppermute | solution.py:17
  394.2 7.7 %collective-permute-start.18 = (f32[1,352,64]{1,2,0:T(8,128)S(1)}, f32[1,352,64]{1,2,0:T(8,128)S(1)}, u32[]{:S(2)}, u32[]{:S(2)}) collective-permute-start(f32[1,352,64]{1,2,0:T(8,128)S(1)} %get-tuple-element.23), channel_id=1, source_target_pairs={{0,16},{16,32},{32,48},{48,64},{64,80},{80,96},{96,112},{112,128},... | collective-permute-start | bytes 270344 | tf_op jit(solution)/shard_map/ppermute | solution.py:17
  397.3 5.4 collective-permute-start.19
  398.6 5.9 %collective-permute-start.17 = (f32[1,352,64]{1,2,0:T(8,128)S(1)}, f32[1,352,64]{1,2,0:T(8,128)S(1)}, u32[]{:S(2)}, u32[]{:S(2)}) collective-permute-start(f32[1,352,64]{1,2,0:T(8,128)S(1)} %get-tuple-element.25), channel_id=1, source_target_pairs={{1,0},{2,1},{3,2},{4,3},{5,4},{6,5},{7,6},{8,7},{9,8},{10,9},{11,1... | collective-permute-start | bytes 270344 | tf_op jit(solution)/shard_map/ppermute | solution.py:18
  424.1 4.8 collective-permute-start.20
  426.2 5.9 %collective-permute-start.21 = (f32[1,352,64]{1,2,0:T(8,128)S(1)}, f32[1,352,64]{1,2,0:T(8,128)S(1)}, u32[]{:S(2)}, u32[]{:S(2)}) collective-permute-start(f32[1,352,64]{1,2,0:T(8,128)S(1)} %get-tuple-element.45), channel_id=1, source_target_pairs={{1,0},{2,1},{3,2},{4,3},{5,4},{6,5},{7,6},{8,7},{9,8},{10,9},{11,1... | collective-permute-start | bytes 270344 | tf_op jit(solution)/shard_map/ppermute | solution.py:18
